TPU v7x, 256 devices: a whole 4x4x8 slice. The times are simulated.
256 devices in a mesh: grp: 8 (over y, x_lo), brick: 32 (over z, x_hi, core).
Axes of the slice: x: 4 (x_hi: 2, x_lo: 2; x = x_hi * 2 + x_lo), y: 4, z: 8, core: 2. Of those that a mesh axis runs over, the one named last changes fastest.
Arguments:
- coeffs: bfloat16 [8, 16384, 1024], P(None, 'brick'), may hold values from -6 to 6
- tensor: bfloat16 [32, 1024, 1024], P('grp', 'brick'), may hold values from -0.005859375 to 0.005859375
- pairs: int32 [2, 2], replicated, may hold values from 0 to 7
- lateral: int32 [16384], P('brick'), may hold values from 0 to 511
- thermal: float32 [8], replicated, may hold values from 0.5 to 1
Outputs:
- updated: float32 [32, 8, 16384], P(None, None, 'brick')
Inputs may be any that keep to these rules, and one draw needn't show every extreme that they name: `pairs`: row p names the species that receives the collision term and the species it collides with. A cell's lateral partner, as an index within the same block of 512 cells.
All inputs are finite; a program needn't handle non-finite values.
Results may differ from a plain program's by a relative error of at most 0.0003.
Values may be sent and summed in bfloat16 or wider, within the bound.
No kernel may reach another device: no remote copies, remote signals or barrier semaphores. Data moves between devices by JAX's collectives and lax.ppermute only.
A program may use at most 128 MiB of HBM per device.

v0:
```python
import jax
import jax.numpy as jnp
from jax import lax
from jax.sharding import PartitionSpec as P

PLANE = 128
collision_update = 0.5
courant = 0.08
max_speed = 11.0
mixing = 0.2


def sent_to_all(array, axis):
    copies = jnp.broadcast_to(array, (lax.axis_size(axis), *array.shape))
    return lax.all_to_all(copies, axis, split_axis=0, concat_axis=0, tiled=True)


def in_order(parts, dim):
    shape = list(parts.shape[1:])
    shape[dim] *= parts.shape[0]
    return jnp.moveaxis(parts, 0, dim).reshape(shape)


def gather_directly(array, axis, dim):
    parts = sent_to_all(array, axis)
    return in_order(parts, dim)


def with_halo(cells, sides, width):
    for axis, dim in sides:
        count = lax.axis_size(axis)
        head = lax.slice_in_dim(cells, 0, width, axis=dim)
        tail = lax.slice_in_dim(cells, cells.shape[dim] - width, cells.shape[dim], axis=dim)
        cells = jnp.concatenate(
            [
                lax.ppermute(tail, axis, [(i, (i + 1) % count) for i in range(count)]),
                cells,
                lax.ppermute(head, axis, [((i + 1) % count, i) for i in range(count)]),
            ],
            axis=dim,
        )
    return cells


def advance(extended, thermal, partner):
    mode_count = extended.shape[0] - 2
    thermo = thermal[None, :, None, None]
    orders = jnp.arange(mode_count, dtype=jnp.int32).astype(jnp.float32)[:, None, None, None]
    speed = thermo * (
        jnp.sqrt(orders) * extended[:mode_count] + jnp.sqrt(orders + 1.0) * extended[2:]
    )
    middle = extended[1 : mode_count + 1]
    face = 0.5 * (speed[:, :, :-1] + speed[:, :, 1:]) - 0.5 * max_speed * thermo * (
        middle[:, :, 1:] - middle[:, :, :-1]
    )
    center = middle[:, :, 1:-1]
    shape_flat = (mode_count, center.shape[1], center.shape[2] * center.shape[3])
    center = center.reshape(shape_flat)
    divergence = (face[:, :, 1:] - face[:, :, :-1]).reshape(shape_flat)
    beside = jnp.take(center, partner, axis=2)
    return center - courant * divergence + mixing * (beside - center)


def local(coeffs, tensor, pairs, lateral, thermal):
    species, cells, width = coeffs.shape
    local_modes = tensor.shape[0]
    group_count = lax.axis_size("grp")
    modes = local_modes * group_count
    pair_count = pairs.shape[0]
    layers = cells // PLANE
    left_rows = jnp.transpose(coeffs[pairs[:, 0]], (2, 0, 1))
    right_flat = coeffs[pairs[:, 1]].reshape(pair_count * cells, width)
    brick_window = jnp.transpose(coeffs[:, :, :modes], (2, 0, 1))
    padded_state = jnp.pad(brick_window, ((1, 1), (0, 0), (0, 0)))
    indicator_matrix = (
        pairs[:, 0][:, None] == jnp.arange(species, dtype=jnp.int32)[None, :]
    ).astype(jnp.float32)
    piece = lax.all_gather(tensor, "brick", axis=1, tiled=True)
    rows_here = piece.shape[1]
    inner = lax.dot_general(
        piece.reshape(local_modes * rows_here, width),
        right_flat,
        (((1,), (1,)), ((), ())),
        preferred_element_type=jnp.float32,
    )
    inner = inner.reshape(local_modes, rows_here, pair_count, cells)
    factor = left_rows.astype(jnp.float32)
    collide = jnp.sum(inner * factor[None], axis=1)
    pair_all = gather_directly(collide, "grp", 0)
    pair_extended = jnp.pad(pair_all, ((1, 1), (0, 0), (0, 0)))
    span = pair_extended.shape[0]
    collision_extended = jnp.einsum(
        "quw,ut->qtw", pair_extended, indicator_matrix, precision=lax.Precision.HIGHEST
    )
    species_state = padded_state.astype(jnp.float32) + collision_update * collision_extended
    extended = with_halo(species_state.reshape(span, species, layers, PLANE), (("brick", 2),), 1)
    updated = advance(extended, thermal, lateral)
    return updated


def solution(mesh):
    in_specs = (P(None, "brick", None), P("grp", "brick", None), P(), P("brick"), P())
    out_specs = P(None, None, "brick")
    return jax.shard_map(local, mesh=mesh, in_specs=in_specs, out_specs=out_specs, check_vma=False)
```

profile of v0, /device:TPU:2, one launch (start us, length us, event | category | flops | bytes accessed | tf_op | source)
XLA Modules:
  0.0 193.8 jit_solution(13047162379919570659)
XLA Ops:
  6.5 0.7 all-gather.2.cloned.1.call-update
  7.3 1.0 slice_reduce_fusion
  8.3 5.5 %gather_fusion = bf16[2,512,1024]{2,1,0:T(8,128)(2,1)} fusion(bf16[8,512,1024]{2,1,0:T(8,128)(2,1)} %param.5, s32[1024]{0:T(1024)S(1)} %get-tuple-element.11), kind=kCustom, calls=%fused_computation | custom fusion | bytes 4194312 | tf_op jit(solution)/shard_map/gather | solution.py:72
  13.8 4.1 %gather_fusion.1 = bf16[2,512,1024]{2,1,0:T(8,128)(2,1)S(1)} fusion(bf16[8,512,1024]{2,1,0:T(8,128)(2,1)} %param.5, s32[1024]{0:T(1024)S(1)} %get-tuple-element.10), kind=kCustom, calls=%fused_computation.1 | custom fusion | bytes 4194312 | tf_op jit(solution)/shard_map/gather | solution.py:71
  17.8 0.5 copy.14
  18.4 2.5 %convert_bitcast_fusion = f32[1024,2,512]{0,2,1:T(8,128)} fusion(bf16[2,512,1024]{2,1,0:T(8,128)(2,1)S(1)} %gather_fusion.1), kind=kLoop, calls=%fused_computation.5 | loop fusion | flops 1048576 | bytes 6291456 | tf_op jit(solution)/shard_map/convert_element_type | solution.py:87
  20.9 92.7 %all-gather.2.cloned.1.call-done = bf16[4,1024,1024]{2,1,0:T(8,128)(2,1)} async-done(((bf16[4,32,1024]{2,1,0:T(8,128)(2,1)}), bf16[4,1024,1024]{2,1,0:T(8,128)(2,1)}) %all-gather.2.cloned.1.call-update) | async-done | bytes 8388624 | tf_op jit(solution)/shard_map/all_gather | solution.py:78
  113.7 16.0 %convolution_bitcast_fusion = f32[4096,1024]{0,1:T(8,128)} fusion(bf16[1024,1024]{1,0:T(8,128)(2,1)} %bitcast.35, bf16[4096,1024]{1,0:T(8,128)(2,1)} %bitcast.38), kind=kOutput, calls=%fused_computation.4 | convolution fusion | flops 8589934592 | bytes 27262976 | tf_op jit(solution)/shard_map/dot_general | solution.py:80
  129.7 20.4 %reshape.44 = f32[4,1024,2,512]{1,0,3,2:T(4,128)} reshape(f32[4096,1024]{0,1:T(8,128)} %convolution_bitcast_fusion) | data formatting | bytes 33554432 | tf_op jit(solution)/shard_map/reshape | solution.py:86
  150.1 10.5 %multiply_reduce_fusion = f32[4,2,512]{0,2,1:T(8,128)S(1)} fusion(f32[4,1024,2,512]{1,0,3,2:T(4,128)} %reshape.44, f32[1024,2,512]{0,2,1:T(8,128)} %convert_bitcast_fusion), kind=kLoop, calls=%fused_computation.3 | loop fusion | flops 8384512 | bytes 20987904 | tf_op jit(solution)/shard_map/reduce_sum | solution.py:88
  160.7 0.2 copy.11
  160.9 0.7 broadcast_in_dim.21
  161.6 5.7 %all-to-all-start = ((f32[8,4,2,512]{3,2,1,0:T(2,128)}), f32[8,4,2,512]{3,2,1,0:T(2,128)S(1)}, u32[]{:S(2)}, u32[]{:S(2)}) async-start(f32[8,4,2,512]{3,2,1,0:T(2,128)} %broadcast_in_dim.21), calls=%async_computation | async-start | bytes 262144 | tf_op jit(solution)/shard_map/all_to_all | solution.py:15
  167.3 5.4 %all-to-all-done = f32[8,4,2,512]{3,2,1,0:T(2,128)S(1)} async-done(((f32[8,4,2,512]{3,2,1,0:T(2,128)}), f32[8,4,2,512]{3,2,1,0:T(2,128)S(1)}, u32[]{:S(2)}, u32[]{:S(2)}) %all-to-all-start) | async-done | bytes 131104 | tf_op jit(solution)/shard_map/all_to_all | solution.py:15
  172.7 0.5 fusion.1
  173.3 0.7 fusion.21
  174.0 5.4 %collective-permute-start.1 = (f32[34,8,1,128]{3,1,2,0:T(8,128)}, f32[34,8,1,128]{3,1,2,0:T(8,128)S(1)}, u32[]{:S(2)}, u32[]{:S(2)}) collective-permute-start(f32[34,8,1,128]{3,1,2,0:T(8,128)} %get-tuple-element.8), channel_id=1, source_target_pairs={{1,0},{2,1},{3,2},{4,3},{5,4},{6,5},{7,6},{8,7},{9,8},{10,9},{11,1... | collective-permute-start | bytes 417800 | tf_op jit(solution)/shard_map/ppermute | solution.py:38
  179.4 0.8 copy.12
  180.3 2.7 %gather_fusion.2 = f32[512,32,8]{1,2,0:T(8,128)} fusion(f32[32,8,512]{0,1,2:T(8,128)S(1)} %copy.12, s32[1024]{0:T(1024)S(1)} %pad_clamp_fusion), kind=kCustom, calls=%fused_computation.2 | custom fusion | bytes 1050624 | tf_op jit(solution)/shard_map/jit(_take)/gather | solution.py:60
  183.0 2.4 %copy.13 = f32[512,32,8]{0,2,1:T(8,128)S(1)} copy(f32[512,32,8]{1,2,0:T(8,128)} %gather_fusion.2) | data formatting | bytes 1048576 | tf_op jit(solution)/shard_map/jit(_take)/gather | solution.py:60
  185.4 0.1 pad_maximum_fusion
  185.5 0.2 fusion.3
  185.7 0.3 fusion.6
  186.0 1.0 fusion.11
  (17 shorter events, 0.1 us)
Async XLA Ops:
  6.5 107.1 %all-gather.2.cloned.1.call-start = ((), (), s32[]{:S(2)}) async-start(), calls=%async_computation.1 | async-start | bytes 8650752 | tf_op jit(solution)/shard_map/all_gather | solution.py:78
  8.2 9.6 %slice-start = ((bf16[8,512,1024]{2,1,0:T(8,128)(2,1)}), bf16[8,512,32]{2,1,0:T(8,128)(2,1)S(1)}, s32[]{:S(2)}) async-start(bf16[8,512,1024]{2,1,0:T(8,128)(2,1)} %param.5), calls=%async_computation.2 | async-start | bytes 2097152 | tf_op jit(solution)/shard_map/slice | solution.py:73
  8.3 10.1 %copy-start = (s32[512]{0:T(512)S(1)}, s32[512]{0:T(512)}, u32[]{:S(2)}) copy-start(s32[512]{0:T(512)} %param.8) | copy-start | bytes 6148
  150.1 17.2 %copy-start.1 = (f32[8]{0:T(128)S(1)}, f32[8]{0:T(128)}, u32[]{:S(2)}) copy-start(f32[8]{0:T(128)} %param.9) | copy-start | bytes 100
  161.6 11.2 %all-to-all-start = ((f32[8,4,2,512]{3,2,1,0:T(2,128)}), f32[8,4,2,512]{3,2,1,0:T(2,128)S(1)}, u32[]{:S(2)}, u32[]{:S(2)}) async-start(f32[8,4,2,512]{3,2,1,0:T(2,128)} %broadcast_in_dim.21), calls=%async_computation | async-start | bytes 262144 | tf_op jit(solution)/shard_map/all_to_all | solution.py:15
  174.0 11.4 %collective-permute-start = (f32[34,8,1,128]{3,1,2,0:T(8,128)}, f32[34,8,1,128]{3,1,2,0:T(8,128)S(1)}, u32[]{:S(2)}, u32[]{:S(2)}) collective-permute-start(f32[34,8,1,128]{3,1,2,0:T(8,128)} %get-tuple-element.9), channel_id=1, source_target_pairs={{0,1},{1,2},{2,3},{3,4},{4,5},{5,6},{6,7},{7,8},{8,9},{9,10},{10,1... | collective-permute-start | bytes 417800 | tf_op jit(solution)/shard_map/ppermute | solution.py:36
  174.0 11.4 %collective-permute-start.1 = (f32[34,8,1,128]{3,1,2,0:T(8,128)}, f32[34,8,1,128]{3,1,2,0:T(8,128)S(1)}, u32[]{:S(2)}, u32[]{:S(2)}) collective-permute-start(f32[34,8,1,128]{3,1,2,0:T(8,128)} %get-tuple-element.8), channel_id=1, source_target_pairs={{1,0},{2,1},{3,2},{4,3},{5,4},{6,5},{7,6},{8,7},{9,8},{10,9},{11,1... | collective-permute-start | bytes 417800 | tf_op jit(solution)/shard_map/ppermute | solution.py:38
Sparse Core Ops, SparseCore 0:
  10.2 103.4 all-gather.1
where the time goes:
time: 195 us; the launch traced here: 194 us
  waiting for transfers between devices  98.9 us (51%)
  local copies, waits for them, and re-layouts  38.2 us (20%)
  matrix products  16.6 us (9%)
  other arithmetic  15.5 us (8%)
  between operations  13.5 us (7%)
  starting transfers between devices  11.1 us (6%)
    all_gather x1, waiting for transfers between devices, local(): piece = lax.all_gather(tensor, 'brick', axis=1, tiled=True)  92.7 us
    reshape x1, local copies, waits for them, and re-layouts, local(): inner = inner.reshape(local_modes, rows_here, pair_count, cells)  20.4 us
    dot_general x1, matrix products, local(): lax.dot_general(piece.reshape(local_modes * rows_here, width), right_flat...  16 us
    reduce_sum x1, other arithmetic, local(): collide = jnp.sum(inner * factor[None], axis=1)  10.5 us
    all_to_all x1, starting transfers between devices, sent_to_all(): return lax.all_to_all(copies, axis, split_axis=0, concat_axis=0, tiled=True)  5.74 us
    gather x1, local copies, waits for them, and re-layouts, local(): right_flat = coeffs[pairs[:, 1]].reshape(pair_count * cells, width)  5.5 us
    all_to_all x1, waiting for transfers between devices, sent_to_all(): return lax.all_to_all(copies, axis, split_axis=0, concat_axis=0, tiled=True)  5.41 us
    ppermute x1, starting transfers between devices, with_halo(): lax.ppermute(head, axis, [((i + 1) % count, i) for i in range(count)])  5.36 us
  transfers between devices with their start and end apart: 4, of which 2 were waited for; matrix products, arithmetic and copies ran while one was open for 10% of the time, Pallas kernels for 0%

commit v1 on v0

--- a/solution.py
+++ b/solution.py
@@ -75,7 +75,8 @@
     indicator_matrix = (
         pairs[:, 0][:, None] == jnp.arange(species, dtype=jnp.int32)[None, :]
     ).astype(jnp.float32)
-    piece = lax.all_gather(tensor, "brick", axis=1, tiled=True)
+    outgoing = jnp.stack([tensor] * lax.axis_size("brick"))
+    piece = jnp.concatenate(lax.all_to_all(outgoing, "brick", 0, 0), axis=1)
     rows_here = piece.shape[1]
     inner = lax.dot_general(
         piece.reshape(local_modes * rows_here, width),

time: 195 us -> 284 us (1.46)
  waiting for transfers between devices: 98.9 us -> 179 us
  local copies, waits for them, and re-layouts: 38.2 us -> 51.8 us
  between operations: 13.5 us -> 0.18 us
  starting transfers between devices: 11.1 us -> 22 us
    all_to_all x0 -> x1, waiting for transfers between devices: none -> 174 us  [local(): piece = jnp.concatenate(lax.all_to_all(outgoing, 'brick', 0, 0), axis=1)]
    all_gather x1 -> x0, waiting for transfers between devices: 92.7 us -> none  [local(): piece = lax.all_gather(tensor, 'brick', axis=1, tiled=True)]
    all_to_all x0 -> x1, starting transfers between devices: none -> 10.7 us  [local(): piece = jnp.concatenate(lax.all_to_all(outgoing, 'brick', 0, 0), axis=1)]
    all_to_all x0 -> x1, local copies, waits for them, and re-layouts: none -> 8.46 us  [local(): piece = jnp.concatenate(lax.all_to_all(outgoing, 'brick', 0, 0), axis=1)]
    another operation x0 -> x1, local copies, waits for them, and re-layouts: none -> 5.24 us  [local(): outgoing = jnp.stack([tensor] * lax.axis_size('brick'))]
  transfers between devices with their start and end apart: 4 -> 4, of which waited for: 2 -> 2; matrix products, arithmetic and copies ran while one was open for 10% -> 7% of each run, Pallas kernels for 0% -> 0%
where the time goes in v1:
time: 284 us; the launch traced here: 283 us
  waiting for transfers between devices  179 us (63%)
  local copies, waits for them, and re-layouts  51.8 us (18%)
  starting transfers between devices  22 us (8%)
  matrix products  15 us (5%)
  other arithmetic  14.8 us (5%)
    all_to_all x1, waiting for transfers between devices, local(): piece = jnp.concatenate(lax.all_to_all(outgoing, 'brick', 0, 0), axis=1)  174 us
    reshape x1, local copies, waits for them, and re-layouts, local(): inner = inner.reshape(local_modes, rows_here, pair_count, cells)  20.4 us
    dot_general x1, matrix products, local(): lax.dot_general(piece.reshape(local_modes * rows_here, width), right_flat...  14.5 us
    all_to_all x1, starting transfers between devices, local(): piece = jnp.concatenate(lax.all_to_all(outgoing, 'brick', 0, 0), axis=1)  10.7 us
    reduce_sum x1, other arithmetic, local(): collide = jnp.sum(inner * factor[None], axis=1)  10.5 us
    all_to_all x1, local copies, waits for them, and re-layouts, local(): piece = jnp.concatenate(lax.all_to_all(outgoing, 'brick', 0, 0), axis=1)  8.46 us
    all_to_all x1, starting transfers between devices, sent_to_all(): return lax.all_to_all(copies, axis, split_axis=0, concat_axis=0, tiled=True)  5.93 us
  transfers between devices with their start and end apart: 4, of which 2 were waited for; matrix products, arithmetic and copies ran while one was open for 7% of the time, Pallas kernels for 0%

profile of v1, /device:TPU:2, one launch (start us, length us, event | category | flops | bytes accessed | tf_op | source)
XLA Modules:
  0.0 283.0 jit_solution(6457531115935615496)
XLA Ops:
  0.0 5.2 %stack.2 = bf16[32,4,32,1024]{3,2,1,0:T(8,128)(2,1)} broadcast(bf16[4,32,1024]{2,1,0:T(8,128)(2,1)} %param.6), dimensions={1,2,3} | broadcast | bytes 8650752 | tf_op jit(solution)/shard_map/stack | solution.py:78
  5.2 10.7 %all-to-all-start = ((bf16[32,4,32,1024]{3,2,1,0:T(8,128)(2,1)}), bf16[32,4,32,1024]{3,2,1,0:T(8,128)(2,1)}, u32[]{:S(2)}, u32[]{:S(2)}) async-start(bf16[32,4,32,1024]{3,2,1,0:T(8,128)(2,1)} %stack.2), calls=%async_computation | async-start | bytes 16777216 | tf_op jit(solution)/shard_map/all_to_all | solution.py:79
  16.2 5.5 %gather_fusion = bf16[2,512,1024]{2,1,0:T(8,128)(2,1)} fusion(bf16[8,512,1024]{2,1,0:T(8,128)(2,1)} %param.5, s32[1024]{0:T(1024)S(1)} %get-tuple-element.11), kind=kCustom, calls=%fused_computation | custom fusion | bytes 4194312 | tf_op jit(solution)/shard_map/gather | solution.py:72
  21.6 4.1 %gather_fusion.1 = bf16[2,512,1024]{2,1,0:T(8,128)(2,1)S(1)} fusion(bf16[8,512,1024]{2,1,0:T(8,128)(2,1)} %param.5, s32[1024]{0:T(1024)S(1)} %get-tuple-element.10), kind=kCustom, calls=%fused_computation.1 | custom fusion | bytes 4194312 | tf_op jit(solution)/shard_map/gather | solution.py:71
  25.7 0.5 copy.15
  26.3 2.5 convert_bitcast_fusion
  28.8 173.8 %all-to-all-done = bf16[32,4,32,1024]{3,2,1,0:T(8,128)(2,1)} async-done(((bf16[32,4,32,1024]{3,2,1,0:T(8,128)(2,1)}), bf16[32,4,32,1024]{3,2,1,0:T(8,128)(2,1)}, u32[]{:S(2)}, u32[]{:S(2)}) %all-to-all-start) | async-done | bytes 8388640 | tf_op jit(solution)/shard_map/all_to_all | solution.py:79
  202.6 8.5 %copy.11 = bf16[32,4,32,1024]{3,2,0,1:T(8,128)(2,1)} copy(bf16[32,4,32,1024]{3,2,1,0:T(8,128)(2,1)} %all-to-all-done) | data formatting | bytes 16777216 | tf_op jit(solution)/shard_map/all_to_all | solution.py:79
  211.1 14.5 %convolution_bitcast_fusion = f32[4096,1024]{0,1:T(8,128)} fusion(bf16[1024,1024]{1,0:T(8,128)(2,1)S(1)} %bitcast.38, bf16[4096,1024]{1,0:T(8,128)(2,1)} %bitcast.37), kind=kOutput, calls=%fused_computation.4 | convolution fusion | flops 8589934592 | bytes 27262976 | tf_op jit(solution)/shard_map/dot_general | solution.py:81
  225.6 20.4 %reshape.46 = f32[4,1024,2,512]{1,0,3,2:T(4,128)} reshape(f32[4096,1024]{0,1:T(8,128)} %convolution_bitcast_fusion) | data formatting | bytes 33554432 | tf_op jit(solution)/shard_map/reshape | solution.py:87
  246.0 10.5 %multiply_reduce_fusion = f32[4,2,512]{0,2,1:T(8,128)S(1)} fusion(f32[4,1024,2,512]{1,0,3,2:T(4,128)} %reshape.46, f32[1024,2,512]{0,2,1:T(8,128)} %convert_bitcast_fusion), kind=kLoop, calls=%fused_computation.3 | loop fusion | flops 8384512 | bytes 20987904 | tf_op jit(solution)/shard_map/reduce_sum | solution.py:89
  256.6 0.2 copy.12
  256.8 0.7 broadcast_in_dim.21
  257.5 5.9 %all-to-all-start.1 = ((f32[8,4,2,512]{3,2,1,0:T(2,128)}), f32[8,4,2,512]{3,2,1,0:T(2,128)S(1)}, u32[]{:S(2)}, u32[]{:S(2)}) async-start(f32[8,4,2,512]{3,2,1,0:T(2,128)} %broadcast_in_dim.21), calls=%async_computation.1 | async-start | bytes 262144 | tf_op jit(solution)/shard_map/all_to_all | solution.py:15
  263.4 5.4 %all-to-all-done.1 = f32[8,4,2,512]{3,2,1,0:T(2,128)S(1)} async-done(((f32[8,4,2,512]{3,2,1,0:T(2,128)}), f32[8,4,2,512]{3,2,1,0:T(2,128)S(1)}, u32[]{:S(2)}, u32[]{:S(2)}) %all-to-all-start.1) | async-done | bytes 131104 | tf_op jit(solution)/shard_map/all_to_all | solution.py:15
  268.8 0.5 fusion.1
  269.3 0.7 fusion.21
  270.1 5.4 %collective-permute-start.1 = (f32[34,8,1,128]{3,1,2,0:T(8,128)}, f32[34,8,1,128]{3,1,2,0:T(8,128)S(1)}, u32[]{:S(2)}, u32[]{:S(2)}) collective-permute-start(f32[34,8,1,128]{3,1,2,0:T(8,128)} %get-tuple-element.8), channel_id=1, source_target_pairs={{1,0},{2,1},{3,2},{4,3},{5,4},{6,5},{7,6},{8,7},{9,8},{10,9},{11,1... | collective-permute-start | bytes 417800 | tf_op jit(solution)/shard_map/ppermute | solution.py:38
  275.5 0.8 copy.13
  276.3 2.7 gather_fusion.2
  279.1 2.4 copy.14
  281.5 0.2 fusion.3
  281.7 0.3 fusion.6
  282.0 1.0 fusion.11
  (22 shorter events, 0.3 us)
Async XLA Ops:
  5.2 10.7 %copy-start.2 = (s32[2,2]{1,0:T(2,128)S(1)}, s32[2,2]{1,0:T(2,128)}, u32[]{:S(2)}) copy-start(s32[2,2]{1,0:T(2,128)} %param.7) | copy-start | bytes 52
  5.2 197.4 %all-to-all-start = ((bf16[32,4,32,1024]{3,2,1,0:T(8,128)(2,1)}), bf16[32,4,32,1024]{3,2,1,0:T(8,128)(2,1)}, u32[]{:S(2)}, u32[]{:S(2)}) async-start(bf16[32,4,32,1024]{3,2,1,0:T(8,128)(2,1)} %stack.2), calls=%async_computation | async-start | bytes 16777216 | tf_op jit(solution)/shard_map/all_to_all | solution.py:79
  16.1 9.6 %slice-start = ((bf16[8,512,1024]{2,1,0:T(8,128)(2,1)}), bf16[8,512,32]{2,1,0:T(8,128)(2,1)S(1)}, s32[]{:S(2)}) async-start(bf16[8,512,1024]{2,1,0:T(8,128)(2,1)} %param.5), calls=%async_computation.2 | async-start | bytes 2097152 | tf_op jit(solution)/shard_map/slice | solution.py:73
  16.1 10.1 %copy-start.1 = (s32[512]{0:T(512)S(1)}, s32[512]{0:T(512)}, u32[]{:S(2)}) copy-start(s32[512]{0:T(512)} %param.8) | copy-start | bytes 6148
  28.8 182.3 %copy-start = (bf16[2,512,1024]{2,1,0:T(8,128)(2,1)S(1)}, bf16[2,512,1024]{2,1,0:T(8,128)(2,1)}, u32[]{:S(2)}) copy-start(bf16[2,512,1024]{2,1,0:T(8,128)(2,1)} %gather_fusion) | copy-start | bytes 6291460
  246.0 17.4 %copy-start.3 = (f32[8]{0:T(128)S(1)}, f32[8]{0:T(128)}, u32[]{:S(2)}) copy-start(f32[8]{0:T(128)} %param.9) | copy-start | bytes 100
  257.5 11.3 %all-to-all-start.1 = ((f32[8,4,2,512]{3,2,1,0:T(2,128)}), f32[8,4,2,512]{3,2,1,0:T(2,128)S(1)}, u32[]{:S(2)}, u32[]{:S(2)}) async-start(f32[8,4,2,512]{3,2,1,0:T(2,128)} %broadcast_in_dim.21), calls=%async_computation.1 | async-start | bytes 262144 | tf_op jit(solution)/shard_map/all_to_all | solution.py:15
  270.1 11.4 %collective-permute-start = (f32[34,8,1,128]{3,1,2,0:T(8,128)}, f32[34,8,1,128]{3,1,2,0:T(8,128)S(1)}, u32[]{:S(2)}, u32[]{:S(2)}) collective-permute-start(f32[34,8,1,128]{3,1,2,0:T(8,128)} %get-tuple-element.9), channel_id=1, source_target_pairs={{0,1},{1,2},{2,3},{3,4},{4,5},{5,6},{6,7},{7,8},{8,9},{9,10},{10,1... | collective-permute-start | bytes 417800 | tf_op jit(solution)/shard_map/ppermute | solution.py:36
  270.1 11.4 %collective-permute-start.1 = (f32[34,8,1,128]{3,1,2,0:T(8,128)}, f32[34,8,1,128]{3,1,2,0:T(8,128)S(1)}, u32[]{:S(2)}, u32[]{:S(2)}) collective-permute-start(f32[34,8,1,128]{3,1,2,0:T(8,128)} %get-tuple-element.8), channel_id=1, source_target_pairs={{1,0},{2,1},{3,2},{4,3},{5,4},{6,5},{7,6},{8,7},{9,8},{10,9},{11,1... | collective-permute-start | bytes 417800 | tf_op jit(solution)/shard_map/ppermute | solution.py:38
